TPU v7x, 128 devices: a whole 4x4x4 slice. The times are simulated.
128 devices in a mesh: row: 8 (over y, x_lo), col: 16 (over z, x_hi, core).
Axes of the slice: x: 4 (x_hi: 2, x_lo: 2; x = x_hi * 2 + x_lo), y: 4, z: 4, core: 2. Of those that a mesh axis runs over, the one named last changes fastest.
Arguments:
- filtered_bands: bfloat16 [4096, 16384], P(None, ('row', 'col')), may hold values from -0.09375 to 0.09375
Outputs:
- gram_upper: float32 [16384, 16384], P('row', 'col')
All inputs are finite; a program needn't handle non-finite values.
Results may differ from a plain program's by a relative error of at most 0.0003.
Values may be sent and summed in bfloat16 or wider, within the bound.
No kernel may reach another device: no remote copies, remote signals or barrier semaphores. Data moves between devices by JAX's collectives and lax.ppermute only.
A program may use at most 128 MiB of HBM per device.

v0:
```python
import jax
import jax.numpy as jnp
from jax import lax
from jax.sharding import PartitionSpec as P


def from_root(shard, axis, root):
    mine = lax.axis_index(axis) == root
    return lax.psum(jnp.where(mine, shard, jnp.zeros_like(shard)), axis)


def tile_product(left_panel, right_panel):
    return lax.dot_general(
        left_panel, right_panel, (((0,), (0,)), ((), ())), preferred_element_type=jnp.float32
    )


def shards(filtered_bands):
    row_count = lax.axis_size("row")
    col_count = lax.axis_size("col")
    own_bands = filtered_bands.shape[1]
    tile_rows = own_bands * col_count
    tile_cols = own_bands * row_count
    grid_ratio = col_count // row_count
    row_index = lax.axis_index("row")
    col_index = lax.axis_index("col")
    half_rows = filtered_bands.shape[0] // 2
    below_diag = (col_index + 1) * tile_cols <= row_index * tile_rows
    accumulated = jnp.zeros((tile_rows, tile_cols), jnp.float32)
    for summa_step in range(2):
        own_part = filtered_bands[summa_step * half_rows : (summa_step + 1) * half_rows]
        left_panel = lax.all_gather(own_part, "col", axis=1, tiled=True)
        column_piece = lax.dynamic_slice_in_dim(
            left_panel, col_index % grid_ratio * tile_cols, tile_cols, 1
        )
        right_panel = from_root(column_piece, "row", col_index // grid_ratio)
        accumulated = lax.cond(
            below_diag,
            lambda current, lhs, rhs: current,
            lambda current, lhs, rhs: current + tile_product(lhs, rhs),
            accumulated,
            left_panel,
            right_panel,
        )
    global_rows = row_index * tile_rows + lax.broadcasted_iota(jnp.int32, (tile_rows, tile_cols), 0)
    global_cols = col_index * tile_cols + lax.broadcasted_iota(jnp.int32, (tile_rows, tile_cols), 1)
    return jnp.where(global_cols >= global_rows, accumulated, jnp.float32(0.0))


def solution(mesh):
    return jax.shard_map(
        shards,
        mesh=mesh,
        in_specs=(P(None, ("row", "col")),),
        out_specs=P("row", "col"),
        check_vma=False,
    )
```

profile of v0, /device:TPU:1, one launch (start us, length us, event | category | flops | bytes accessed | tf_op | source)
XLA Modules:
  0.0 551.0 jit_solution(9675241699814306321)
XLA Ops:
  6.5 0.0 all-gather.3.cloned.1.call-start
  6.5 2.2 fusion
  8.8 0.0 all-gather.3.cloned.1.call-update
  8.8 0.0 all-gather.5.cloned.1.call-start
  8.8 0.7 all-gather.5.cloned.1.call-update
  9.5 0.0 all-reduce.3.cloned.1.call-start
  9.6 80.2 %all-gather.3.cloned.1.call-done = bf16[2048,2048]{1,0:T(8,128)(2,1)} async-done(((bf16[2048,128]{1,0:T(8,128)(2,1)}), bf16[2048,2048]{1,0:T(8,128)(2,1)}) %all-gather.3.cloned.1.call-update) | async-done | bytes 8388624 | tf_op jit(solution)/shard_map/all_gather | solution.py:32
  89.9 5.4 dynamic-slice_select_fusion.1
  95.3 70.9 %all-gather.5.cloned.1.call-done = bf16[2048,2048]{1,0:T(8,128)(2,1)} async-done(((bf16[2048,128]{1,0:T(8,128)(2,1)}), bf16[2048,2048]{1,0:T(8,128)(2,1)}) %all-gather.5.cloned.1.call-update) | async-done | bytes 8388624 | tf_op jit(solution)/shard_map/all_gather | solution.py:32
  166.2 5.4 dynamic-slice_select_fusion
  171.6 0.0 all-reduce.3.cloned.1.call-update
  171.7 336.4 %all-reduce.3.cloned.1.call-done = (bf16[2048,1024]{1,0:T(8,128)(2,1)}, bf16[2048,1024]{1,0:T(8,128)(2,1)}) async-done(((bf16[2048,1024]{1,0:T(8,128)(2,1)}, bf16[2048,1024]{1,0:T(8,128)(2,1)}), (bf16[2048,1024]{1,0:T(8,128)(2,1)}, bf16[2048,1024]{1,0:T(8,128)(2,1)})) %all-reduce.3.cloned.1.call-update) | async-done | bytes 8388624 | tf_op jit(solution)/shard_map/psum | solution.py:9
  508.0 14.6 %conditional.2 = (f32[2048,1024]{1,0:T(8,128)}) conditional(s32[]{:T(128)} %convert_element_type.4, (bf16[2048,2048]{1,0:T(8,128)(2,1)}, bf16[2048,1024]{1,0:T(8,128)(2,1)}) %tuple.17, () %tuple.18), branch_computations={%region_2.3_spmd, %region_3.4_spmd} | conditional | flops 8589934592 | bytes 20971528 | solution.py:37
  508.0 14.6 %fusion.1 = f32[2048,1024]{1,0:T(8,128)} fusion(bf16[2048,2048]{1,0:T(8,128)(2,1)} %get-tuple-element.22, bf16[2048,1024]{1,0:T(8,128)(2,1)} %get-tuple-element.23), kind=kOutput, calls=%fused_computation.7 | convolution fusion | flops 8589934592 | bytes 20971520 | tf_op jit(solution)/shard_map/cond/branch_0_fun/dot_general | solution.py:13
  522.7 15.8 %conditional.3 = (f32[2048,1024]{1,0:T(8,128)}) conditional(s32[]{:T(128)} %convert_element_type.4, (bf16[2048,2048]{1,0:T(8,128)(2,1)}, bf16[2048,1024]{1,0:T(8,128)(2,1)}, f32[2048,1024]{1,0:T(8,128)}) %tuple.19, f32[2048,1024]{1,0:T(8,128)} %get-tuple-element.33), branch_computations={%region_4.5_spmd, %region_5.6_spmd} | conditional | flops 8592031744 | bytes 29360136 | solution.py:37
  522.7 15.8 %convolution_add_fusion = f32[2048,1024]{1,0:T(8,128)} fusion(f32[2048,1024]{1,0:T(8,128)} %get-tuple-element.24, bf16[2048,2048]{1,0:T(8,128)(2,1)} %get-tuple-element.25, bf16[2048,1024]{1,0:T(8,128)(2,1)} %get-tuple-element.26), kind=kOutput, calls=%fused_computation | convolution fusion | flops 8592031744 | bytes 29360128 | tf_op jit(solution)/shard_map/cond/branch_0_fun/dot_general | solution.py:13
  538.5 5.9 %compare_select_fusion = f32[2048,1024]{1,0:T(8,128)} fusion(f32[2048,1024]{1,0:T(8,128)} %get-tuple-element.34, s32[1024]{0:T(1024)S(1)} %iota_add_fusion.1, s32[2048]{0:T(1024)S(1)} %iota_add_fusion), kind=kLoop, calls=%fused_computation.1 | loop fusion | flops 4194304 | bytes 16789504 | tf_op jit(solution)/shard_map/jit(_where)/select_n | solution.py:47
  (2 shorter events, 0.0 us)
Async XLA Ops:
  6.5 83.3 %all-gather.3.cloned.1.call-start = ((), (), s32[]{:S(2)}) async-start(), calls=%async_computation | async-start | bytes 8912896 | tf_op jit(solution)/shard_map/all_gather | solution.py:32
  8.8 157.4 %all-gather.5.cloned.1.call-start = ((), (), s32[]{:S(2)}) async-start(), calls=%async_computation.1 | async-start | bytes 8912896 | tf_op jit(solution)/shard_map/all_gather | solution.py:32
  9.5 498.5 %all-reduce.3.cloned.1.call-start = ((), (), s32[]{:S(2)}) async-start(), calls=%async_computation.2 | async-start | bytes 16777216 | tf_op jit(solution)/shard_map/psum | solution.py:9
Sparse Core Ops, SparseCore 0:
  9.7 80.1 all-gather.2
  92.2 73.9 all-gather.4
  171.7 336.2 all-reduce.2
where the time goes:
time: 551 us
  waiting for transfers between devices  488 us (89%)
  matrix products  30.5 us (6%)
  other arithmetic  16.8 us (3%)
  between operations  13.2 us (2%)
    psum x1, waiting for transfers between devices, from_root(): return lax.psum(jnp.where(mine, shard, jnp.zeros_like(shard)), axis)  336 us
    all_gather x2, waiting for transfers between devices, shards(): left_panel = lax.all_gather(own_part, 'col', axis=1, tiled=True)  151 us
    dot_general x2, matrix products, tile_product(): lax.dot_general(left_panel, right_panel, (((0,), (0,)), ((), ())), prefer...  30.5 us
  transfers between devices with their start and end apart: 3, of which 3 were waited for; matrix products, arithmetic and copies ran while one was open for 1% of the time, Pallas kernels for 0%

commit v1 on v0

v1 whole, which is shorter than its diff:
```python
import functools

import jax
import jax.numpy as jnp
import numpy as np
from jax import lax
from jax.experimental import pallas as pl
from jax.experimental.pallas import tpu as pltpu
from jax.sharding import PartitionSpec as P


ROWS, COLS = 8, 16
BOTH = ("row", "col")


def coords(device):
    row, col = divmod(device, COLS)
    y, x_lo = divmod(row, 2)
    z, rest = divmod(col, 4)
    x_hi, core = divmod(rest, 2)
    return 2 * x_hi + x_lo, y, z, core


def device_at(x, y, z, core):
    x, y, z = x % 4, y % 4, z % 4
    return (y * 2 + x % 2) * COLS + z * 4 + (x // 2) * 2 + core


def moves(step):
    return {d: device_at(*step(*coords(d))) for d in range(ROWS * COLS)}


def transpose_moves():
    out = {}
    for k in range(ROWS):
        z_to, x_hi_to = divmod(k, 2)
        for s in range(COLS):
            z, x_hi, core = s // 4, (s // 2) % 2, s % 2
            shift = (0, 2, 1, 3)[(z % 2) * 2 + core]
            out[k * COLS + s] = device_at(2 * x_hi_to + (x_hi ^ core), z_to + shift, z_to, z // 2)
    return out


HOPS = (
    ("row_b", lambda x, y, z, c: (x + 2, y, z, c), "row_a", "row_a"),
    ("row_a_up", lambda x, y, z, c: (x, y, z + 1, c), "row_a", "row_a"),
    ("row_a_down", lambda x, y, z, c: (x, y, z - 1, c), "row_a", "row_a"),
    ("row_b_up", lambda x, y, z, c: (x, y, z + 1, c), "row_b", "row_b"),
    ("row_b_down", lambda x, y, z, c: (x, y, z - 1, c), "row_b", "row_b"),
    ("row_a_far", lambda x, y, z, c: (x, y, z + 1 - 2 * c, c), "row_a_up", "row_a_down"),
    ("row_b_far", lambda x, y, z, c: (x, y, z + 1 - 2 * c, c), "row_b_up", "row_b_down"),
    ("col_a", None, "row_a", "row_a"),
    ("col_b", lambda x, y, z, c: (x ^ 1, y, z, c), "col_a", "col_a"),
    ("col_a_up", lambda x, y, z, c: (x, y + 1, z, c), "col_a", "col_a"),
    ("col_a_down", lambda x, y, z, c: (x, y - 1, z, c), "col_a", "col_a"),
    ("col_b_up", lambda x, y, z, c: (x, y + 1, z, c), "col_b", "col_b"),
    ("col_b_down", lambda x, y, z, c: (x, y - 1, z, c), "col_b", "col_b"),
    ("col_a_far", lambda x, y, z, c: (x, y + 1 - 2 * c, z, c), "col_a_up", "col_a_down"),
    ("col_b_far", lambda x, y, z, c: (x ^ 1, y, z, c), "col_a_far", "col_a_far"),
)
ROW_NAMES = ("row_a", "row_b", "row_a_up", "row_a_down", "row_b_up", "row_b_down", "row_a_far", "row_b_far")
COL_NAMES = ("col_a", "col_b", "col_a_up", "col_a_down", "col_b_up", "col_b_down", "col_a_far", "col_b_far")
OTHER_CORE = sorted(moves(lambda x, y, z, c: (x, y, z, 1 - c)).items())


def active(device):
    row, col = divmod(device, COLS)
    return col // 2 >= row


@functools.cache
def plan():
    devices = range(ROWS * COLS)
    full = {n: transpose_moves() if step is None else moves(step) for n, step, _, _ in HOPS}
    holds = {"row_a": {d: d for d in devices}}
    for name, _, core0, core1 in HOPS:
        holds[name] = {t: holds[core1 if s % 2 else core0][s] for s, t in full[name].items()}
    needed = {n: set() for n in holds}
    for d in devices:
        if active(d):
            for n in ROW_NAMES:
                needed[n] |= {d, d ^ 1}
            for n in COL_NAMES:
                needed[n].add(d)
    pairs = {}
    for name, _, core0, core1 in reversed(HOPS):
        pairs[name] = sorted((s, t) for s, t in full[name].items() if t in needed[name])
        for s, _ in pairs[name]:
            needed[core1 if s % 2 else core0].add(s)
    places = np.zeros((ROWS * COLS, 24), np.int32)
    for d in devices:
        row, col = divmod(d, COLS)
        for i, n in enumerate(ROW_NAMES):
            assert holds[n][d] // COLS == row and holds[n][d ^ 1] // COLS == row
            places[d, 2 * i] = holds[n][d] % COLS
            places[d, 2 * i + 1] = holds[n][d ^ 1] % COLS
        for i, n in enumerate(COL_NAMES):
            assert holds[n][d] // COLS == col // 2 and holds[n][d] % COLS // 8 == col % 2
            places[d, 16 + i] = holds[n][d] % 8
        assert len(set(places[d, :16])) == 16 and len(set(places[d, 16:])) == 8
    return pairs, places


def tile_kernel(n_left, n_right, meta, *refs):
    left, right = refs[:n_left], refs[n_left : n_left + n_right]
    out, left_buf, right_buf, stage, left_sem, right_sem, out_sem = refs[-7:]
    n_pairs = n_left // 2
    row0, col0, is_active = meta[n_left + n_right], meta[n_left + n_right + 1], meta[n_left + n_right + 2]

    def left_copy(i):
        return pltpu.make_async_copy(
            left[i], left_buf.at[i // 2, :, pl.ds(i % 2 * 128, 128)], left_sem.at[i]
        )

    def right_copy(j):
        return pltpu.make_async_copy(right[j], right_buf.at[:, pl.ds(j * 128, 128)], right_sem.at[j])

    def out_copy(slot, i, half, j):
        place = meta[2 * i + half]
        return pltpu.make_async_copy(
            stage.at[slot, pl.ds(half * 128, 128), pl.ds(j * 128, 128)],
            out.at[
                pl.ds(pl.multiple_of(place * 128, 128), 128),
                pl.ds(pl.multiple_of(meta[n_left + j] * 128, 128), 128),
            ],
            out_sem.at[slot, half, j],
        )

    def each_out(slot, i, act):
        for half in range(2):
            for j in range(n_right):
                act(out_copy(slot, i, half, j))

    @pl.when(is_active == 1)
    def _():
        for j in range(n_right):
            right_copy(j).start()
        for i in range(n_left):
            left_copy(i).start()
        for j in range(n_right):
            right_copy(j).wait()

    @pl.when(is_active == 0)
    def _():
        stage[...] = jnp.zeros_like(stage)

    @pl.loop(0, n_pairs)
    def _(i):
        slot = i % 2

        @pl.when(i >= 2)
        def _():
            each_out(slot, i - 2, lambda c: c.wait())

        @pl.when(is_active == 1)
        def _():
            for half in range(2):
                pltpu.make_async_copy(
                    left[0], left_buf.at[i, :, pl.ds(half * 128, 128)], left_sem.at[2 * i + half]
                ).wait()
            product = lax.dot_general(
                left_buf[i], right_buf[...], (((0,), (0,)), ((), ())), preferred_element_type=jnp.float32
            )
            ahead = lax.broadcasted_iota(jnp.int32, (128, 128), 1) - lax.broadcasted_iota(jnp.int32, (128, 128), 0)
            for half in range(2):
                for j in range(n_right):
                    lag = row0 + meta[2 * i + half] * 128 - col0 - meta[n_left + j] * 128
                    block = product[half * 128 : half * 128 + 128, j * 128 : j * 128 + 128]
                    stage[slot, half * 128 : half * 128 + 128, j * 128 : j * 128 + 128] = jnp.where(
                        ahead >= lag, block, 0.0
                    )

        each_out(slot, i, lambda c: c.start())

    for i in range(max(n_pairs - 2, 0), n_pairs):
        each_out(i % 2, i, lambda c: c.wait())


def tile_part(meta, left, right, shape, previous=None):
    n_left, n_right = len(left), len(right)
    any_spec = pl.BlockSpec(memory_space=pl.ANY)
    extra = () if previous is None else (previous,)

    def kernel(meta, *refs):
        if extra:
            refs = refs[: n_left + n_right] + refs[n_left + n_right + 1 :]
        tile_kernel(n_left, n_right, meta, *refs)

    return pl.pallas_call(
        kernel,
        out_shape=jax.ShapeDtypeStruct(shape, jnp.float32),
        grid_spec=pltpu.PrefetchScalarGridSpec(
            num_scalar_prefetch=1,
            grid=(1,),
            in_specs=[any_spec] * (n_left + n_right + len(extra)),
            out_specs=any_spec,
            scratch_shapes=[
                pltpu.VMEM((n_left // 2, 4096, 256), jnp.bfloat16),
                pltpu.VMEM((4096, 128 * n_right), jnp.bfloat16),
                pltpu.VMEM((2, 256, 128 * n_right), jnp.float32),
                pltpu.SemaphoreType.DMA((n_left,)),
                pltpu.SemaphoreType.DMA((n_right,)),
                pltpu.SemaphoreType.DMA((2, 2, n_right)),
            ],
        ),
        input_output_aliases={1 + n_left + n_right: 0} if extra else {},
        compiler_params=pltpu.CompilerParams(vmem_limit_bytes=56 << 20),
        cost_estimate=pl.CostEstimate(
            flops=2 * 4096 * 128 * 128 * n_left * n_right,
            bytes_accessed=(n_left + n_right) * 4096 * 128 * 2 + n_left * n_right * 128 * 128 * 4,
            transcendentals=0,
        ),
    )(meta, *left, *right, *extra)


def shards(filtered_bands):
    pairs, places = plan()
    row, col = lax.axis_index("row"), lax.axis_index("col")
    core = col % 2
    shape = (filtered_bands.shape[1] * COLS, filtered_bands.shape[1] * ROWS)
    place = lax.dynamic_index_in_dim(jnp.asarray(places), row * COLS + col, 0, keepdims=False)
    held = {"row_a": filtered_bands}
    for name, _, core0, core1 in HOPS:
        sent = held[core0] if core0 == core1 else jnp.where(core == 0, held[core0], held[core1])
        held[name] = lax.ppermute(sent, BOTH, pairs[name])
    for name in ROW_NAMES:
        held["other_" + name] = lax.ppermute(held[name], BOTH, OTHER_CORE)

    ends = jnp.stack([row * shape[0], col * shape[1], (col // 2 >= row).astype(jnp.int32)])

    def part(row_names, col_names, previous=None):
        left = [h for n in row_names for h in (held[n], held["other_" + n])]
        right = [held[n] for n in col_names]
        picks = [2 * ROW_NAMES.index(n) + o for n in row_names for o in (0, 1)]
        picks += [16 + COL_NAMES.index(n) for n in col_names]
        meta = jnp.concatenate([place[np.array(picks)], ends])
        return tile_part(meta, left, right, shape, previous)

    return part(ROW_NAMES, COL_NAMES)


def solution(mesh):
    return jax.shard_map(
        shards,
        mesh=mesh,
        in_specs=(P(None, ("row", "col")),),
        out_specs=P("row", "col"),
        check_vma=False,
    )
```

time: 551 us -> 170 us (0.31)
  waiting for transfers between devices: 488 us -> 79.7 us
  starting transfers between devices: 0.08 us -> 54 us
  matrix products: 30.5 us -> 0 us
  Pallas kernels: 0 us -> 29.5 us
  other arithmetic: 16.8 us -> 2.24 us
  between operations: 13.2 us -> 0.36 us
    psum x1 -> x0, waiting for transfers between devices: 336 us -> none  [from_root(): return lax.psum(jnp.where(mine, shard, jnp.zeros_like(shard)), axis)]
    all_gather x2 -> x0, waiting for transfers between devices: 151 us -> none  [shards(): left_panel = lax.all_gather(own_part, 'col', axis=1, tiled=True)]
    ppermute x0 -> x23, waiting for transfers between devices: none -> 79.7 us  [the longest x15 79.7 us: shards(): held[name] = lax.ppermute(sent, BOTH, pairs[name])]
    ppermute x0 -> x23, starting transfers between devices: none -> 54 us  [the longest x15 42.5 us: shards(): held[name] = lax.ppermute(sent, BOTH, pairs[name])]
    dot_general x2 -> x0, matrix products: 30.5 us -> none  [tile_product(): lax.dot_general(left_panel, right_panel, (((0,), (0,)), ((), ())), prefer...]
    pallas_call x0 -> x1, Pallas kernels: none -> 29.5 us  [tile_part(): pl.pallas_call(kernel, out_shape=jax.ShapeDtypeStruct(shape, jnp.float32)...]
    select_n x3, other arithmetic: 16.7 us -> 1.57 us  [shards(): jnp.where(core == 0, held[core0], held[core1])]
  transfers between devices with their start and end apart: 3 -> 23, of which waited for: 3 -> 8; matrix products, arithmetic and copies ran while one was open for 1% -> 2% of each run, Pallas kernels for 0% -> 0%
where the time goes in v1:
time: 170 us; the launch traced here: 167 us
  waiting for transfers between devices  79.7 us (47%)
  starting transfers between devices  54 us (32%)
  Pallas kernels  29.5 us (17%)
  other arithmetic  2.24 us (1%)
    ppermute x15, waiting for transfers between devices, shards(): held[name] = lax.ppermute(sent, BOTH, pairs[name])  79.7 us
    ppermute x15, starting transfers between devices, shards(): held[name] = lax.ppermute(sent, BOTH, pairs[name])  42.5 us
    pallas_call x1, Pallas kernels, tile_part(): pl.pallas_call(kernel, out_shape=jax.ShapeDtypeStruct(shape, jnp.float32)...  29.5 us
    ppermute x8, starting transfers between devices, shards(): held['other_' + name] = lax.ppermute(held[name], BOTH, OTHER_CORE)  11.5 us
  transfers between devices with their start and end apart: 23, of which 8 were waited for; matrix products, arithmetic and copies ran while one was open for 2% of the time, Pallas kernels for 0%

profile of v1, /device:TPU:1, one launch (start us, length us, event | category | flops | bytes accessed | tf_op | source)
XLA Modules:
  0.0 167.2 jit_solution(10340226475258977716)
XLA Ops:
  0.0 5.5 %collective-permute-start.1 = (bf16[4096,128]{1,0:T(8,128)(2,1)}, bf16[4096,128]{1,0:T(8,128)(2,1)}, u32[]{:S(2)}, u32[]{:S(2)}) collective-permute-start(bf16[4096,128]{1,0:T(8,128)(2,1)} %refs_0_.1), channel_id=1, source_target_pairs={{0,2},{1,3},{2,0},{3,1},{4,6},{5,7},{6,4},{7,5},{8,10},{9,11},{10,... | collective-permute-start | bytes 3145736 | tf_op jit(solution)/shard_map/ppermute | solution.py:225
  5.5 5.7 %collective-permute-start.15 = (bf16[4096,128]{1,0:T(8,128)(2,1)}, bf16[4096,128]{1,0:T(8,128)(2,1)}, u32[]{:S(2)}, u32[]{:S(2)}) collective-permute-start(bf16[4096,128]{1,0:T(8,128)(2,1)} %refs_0_.1), channel_id=1, source_target_pairs={{0,0},{1,80},{2,16},{3,64},{4,32},{5,112},{6,48},{7,96},{8,1},{9,8... | collective-permute-start | bytes 3145736 | tf_op jit(solution)/shard_map/ppermute | solution.py:225
  11.2 4.2 %collective-permute-start.5 = (bf16[4096,128]{1,0:T(8,128)(2,1)}, bf16[4096,128]{1,0:T(8,128)(2,1)S(1)}, u32[]{:S(2)}, u32[]{:S(2)}) collective-permute-start(bf16[4096,128]{1,0:T(8,128)(2,1)} %refs_0_.1), channel_id=1, source_target_pairs={{0,12},{1,13},{2,14},{3,15},{4,0},{5,1},{6,2},{7,3},{8,4},{9,5},{1... | collective-permute-start | bytes 3145736 | tf_op jit(solution)/shard_map/ppermute | solution.py:225
  15.4 1.9 %collective-permute-start.3 = (bf16[4096,128]{1,0:T(8,128)(2,1)}, bf16[4096,128]{1,0:T(8,128)(2,1)S(1)}, u32[]{:S(2)}, u32[]{:S(2)}) collective-permute-start(bf16[4096,128]{1,0:T(8,128)(2,1)} %refs_0_.1), channel_id=1, source_target_pairs={{0,4},{1,5},{2,6},{3,7},{4,8},{5,9},{6,10},{7,11},{8,12},{9,13},{1... | collective-permute-start | bytes 3145736 | tf_op jit(solution)/shard_map/ppermute | solution.py:225
  17.4 10.9 %collective-permute-done.1.refs_2_ = bf16[4096,128]{1,0:T(8,128)(2,1)} collective-permute-done((bf16[4096,128]{1,0:T(8,128)(2,1)}, bf16[4096,128]{1,0:T(8,128)(2,1)}, u32[]{:S(2)}, u32[]{:S(2)}) %collective-permute-start.1) | collective-permute-done | bytes 1048608 | tf_op jit(solution)/shard_map/ppermute | solution.py:225
  28.2 6.0 %collective-permute-start.9 = (bf16[4096,128]{1,0:T(8,128)(2,1)}, bf16[4096,128]{1,0:T(8,128)(2,1)S(1)}, u32[]{:S(2)}, u32[]{:S(2)}) collective-permute-start(bf16[4096,128]{1,0:T(8,128)(2,1)} %collective-permute-done.1.refs_2_), channel_id=1, source_target_pairs={{0,12},{1,13},{2,14},{3,15},{4,0},{5,1},{6,2},{7,3},{8,4},{9,5},{1... | collective-permute-start | bytes 3145736 | tf_op jit(solution)/shard_map/ppermute | solution.py:225
  34.2 1.9 %collective-permute-start.7 = (bf16[4096,128]{1,0:T(8,128)(2,1)}, bf16[4096,128]{1,0:T(8,128)(2,1)}, u32[]{:S(2)}, u32[]{:S(2)}) collective-permute-start(bf16[4096,128]{1,0:T(8,128)(2,1)} %collective-permute-done.1.refs_2_), channel_id=1, source_target_pairs={{0,4},{1,5},{2,6},{3,7},{4,8},{5,9},{6,10},{7,11},{8,12},{9,13},{1... | collective-permute-start | bytes 3145736 | tf_op jit(solution)/shard_map/ppermute | solution.py:225
  36.2 3.9 %collective-permute-done.15.refs_16_ = bf16[4096,128]{1,0:T(8,128)(2,1)} collective-permute-done((bf16[4096,128]{1,0:T(8,128)(2,1)}, bf16[4096,128]{1,0:T(8,128)(2,1)}, u32[]{:S(2)}, u32[]{:S(2)}) %collective-permute-start.15) | collective-permute-done | bytes 1048608 | tf_op jit(solution)/shard_map/ppermute | solution.py:225
  40.0 1.3 collective-permute-start.18
  41.3 8.7 %collective-permute-done.5.refs_6_ = bf16[4096,128]{1,0:T(8,128)(2,1)S(1)} collective-permute-done((bf16[4096,128]{1,0:T(8,128)(2,1)}, bf16[4096,128]{1,0:T(8,128)(2,1)S(1)}, u32[]{:S(2)}, u32[]{:S(2)}) %collective-permute-start.5) | collective-permute-done | bytes 1048608 | tf_op jit(solution)/shard_map/ppermute | solution.py:225
  50.0 1.3 collective-permute-start.17
  51.3 5.6 %collective-permute-start = (bf16[4096,128]{1,0:T(8,128)(2,1)}, bf16[4096,128]{1,0:T(8,128)(2,1)S(1)}, u32[]{:S(2)}, u32[]{:S(2)}) collective-permute-start(bf16[4096,128]{1,0:T(8,128)(2,1)} %refs_0_.1), channel_id=1, source_target_pairs={{0,1},{1,0},{2,3},{3,2},{4,5},{5,4},{6,7},{7,6},{8,9},{9,8},{10,11... | collective-permute-start | bytes 3145736 | tf_op jit(solution)/shard_map/ppermute | solution.py:227
  57.0 15.5 %collective-permute-done.9.refs_10_ = bf16[4096,128]{1,0:T(8,128)(2,1)S(1)} collective-permute-done((bf16[4096,128]{1,0:T(8,128)(2,1)}, bf16[4096,128]{1,0:T(8,128)(2,1)S(1)}, u32[]{:S(2)}, u32[]{:S(2)}) %collective-permute-start.9) | collective-permute-done | bytes 1048608 | tf_op jit(solution)/shard_map/ppermute | solution.py:225
  72.5 4.8 %collective-permute-start.11 = (bf16[4096,128]{1,0:T(8,128)(2,1)S(1)}, bf16[4096,128]{1,0:T(8,128)(2,1)S(1)}, u32[]{:S(2)}, u32[]{:S(2)}) collective-permute-start(bf16[4096,128]{1,0:T(8,128)(2,1)S(1)} %broadcast_select_fusion.2), channel_id=1, source_target_pairs={{0,4},{1,13},{2,6},{3,15},{4,8},{5,1},{6,10},{7,3},{8,12},{9,5},{1... | collective-permute-start | bytes 3145736 | tf_op jit(solution)/shard_map/ppermute | solution.py:225
  77.9 1.1 collective-permute-start.2
  79.1 1.4 broadcast_select_fusion
  80.5 1.3 collective-permute-start.16
  81.8 7.2 %collective-permute-done.11.refs_12_ = bf16[4096,128]{1,0:T(8,128)(2,1)S(1)} collective-permute-done((bf16[4096,128]{1,0:T(8,128)(2,1)S(1)}, bf16[4096,128]{1,0:T(8,128)(2,1)S(1)}, u32[]{:S(2)}, u32[]{:S(2)}) %collective-permute-start.11) | collective-permute-done | bytes 1048608 | tf_op jit(solution)/shard_map/ppermute | solution.py:225
  89.0 2.0 %collective-permute-start.12 = (bf16[4096,128]{1,0:T(8,128)(2,1)S(1)}, bf16[4096,128]{1,0:T(8,128)(2,1)S(1)}, u32[]{:S(2)}, u32[]{:S(2)}) collective-permute-start(bf16[4096,128]{1,0:T(8,128)(2,1)S(1)} %collective-permute-done.11.refs_12_), channel_id=1, source_target_pairs={{0,1},{1,0},{2,3},{3,2},{4,5},{5,4},{6,7},{7,6},{8,9},{9,8},{10,11... | collective-permute-start | bytes 3145736 | tf_op jit(solution)/shard_map/ppermute | solution.py:227
  91.1 3.5 %collective-permute-start.13 = (bf16[4096,128]{1,0:T(8,128)(2,1)S(1)}, bf16[4096,128]{1,0:T(8,128)(2,1)}, u32[]{:S(2)}, u32[]{:S(2)}) collective-permute-start(bf16[4096,128]{1,0:T(8,128)(2,1)S(1)} %broadcast_select_fusion.1), channel_id=1, source_target_pairs={{0,4},{1,13},{2,6},{3,15},{4,8},{5,1},{6,10},{7,3},{8,12},{9,5},{1... | collective-permute-start | bytes 3145736 | tf_op jit(solution)/shard_map/ppermute | solution.py:225
  94.6 1.3 collective-permute-start.21
  95.9 10.3 %collective-permute-done.16.refs_17_ = bf16[4096,128]{1,0:T(8,128)(2,1)} collective-permute-done((bf16[4096,128]{1,0:T(8,128)(2,1)}, bf16[4096,128]{1,0:T(8,128)(2,1)}, u32[]{:S(2)}, u32[]{:S(2)}) %collective-permute-start.16) | collective-permute-done | bytes 1048608 | tf_op jit(solution)/shard_map/ppermute | solution.py:225
  106.2 2.1 %collective-permute-start.8 = (bf16[4096,128]{1,0:T(8,128)(2,1)}, bf16[4096,128]{1,0:T(8,128)(2,1)}, u32[]{:S(2)}, u32[]{:S(2)}) collective-permute-start(bf16[4096,128]{1,0:T(8,128)(2,1)} %collective-permute-done.7.refs_8_), channel_id=1, source_target_pairs={{0,1},{1,0},{2,3},{3,2},{4,5},{5,4},{6,7},{7,6},{8,9},{9,8},{10,11... | collective-permute-start | bytes 3145736 | tf_op jit(solution)/shard_map/ppermute | solution.py:227
  108.2 1.3 collective-permute-start.20
  109.6 1.3 collective-permute-start.19
  111.0 1.3 collective-permute-start.22
  112.4 0.7 dynamic-slice_bitcast_fusion
  113.1 0.7 gather_fusion
  113.8 0.7 pad_add_fusion.meta
  114.4 20.7 %collective-permute-done.20.refs_21_ = bf16[4096,128]{1,0:T(8,128)(2,1)} collective-permute-done((bf16[4096,128]{1,0:T(8,128)(2,1)}, bf16[4096,128]{1,0:T(8,128)(2,1)}, u32[]{:S(2)}, u32[]{:S(2)}) %collective-permute-start.20) | collective-permute-done | bytes 1048608 | tf_op jit(solution)/shard_map/ppermute | solution.py:225
  135.1 2.5 %collective-permute-done.19.refs_20_ = bf16[4096,128]{1,0:T(8,128)(2,1)} collective-permute-done((bf16[4096,128]{1,0:T(8,128)(2,1)}, bf16[4096,128]{1,0:T(8,128)(2,1)}, u32[]{:S(2)}, u32[]{:S(2)}) %collective-permute-start.19) | collective-permute-done | bytes 1048608 | tf_op jit(solution)/shard_map/ppermute | solution.py:225
  137.7 29.5 %shard_map.46 = f32[2048,1024]{1,0:T(8,128)} custom-call(s32[27]{0:T(128)} %pad_add_fusion.meta, bf16[4096,128]{1,0:T(8,128)(2,1)} %refs_0_.1, bf16[4096,128]{1,0:T(8,128)(2,1)} %copy-done.3, bf16[4096,128]{1,0:T(8,128)(2,1)} %collective-permute-done.1.refs_2_, bf16[4096,128]{1,0:T(8,128)(2,1)} %copy-done.7, bf16[4096,128]{1,0:T(8,128)(2,1)} %copy-done.1, ...), custom_call_target="tpu_custom_call" | custom-call | flops 17179869184 | bytes 33554432 | tf_op jit(solution)/shard_map/pallas_call | solution.py:189
  (43 shorter events, 1.1 us)
Async XLA Ops:
  0.0 28.2 %collective-permute-start.1 = (bf16[4096,128]{1,0:T(8,128)(2,1)}, bf16[4096,128]{1,0:T(8,128)(2,1)}, u32[]{:S(2)}, u32[]{:S(2)}) collective-permute-start(bf16[4096,128]{1,0:T(8,128)(2,1)} %refs_0_.1), channel_id=1, source_target_pairs={{0,2},{1,3},{2,0},{3,1},{4,6},{5,7},{6,4},{7,5},{8,10},{9,11},{10,... | collective-permute-start | bytes 3145736 | tf_op jit(solution)/shard_map/ppermute | solution.py:225
  5.5 34.6 %collective-permute-start.15 = (bf16[4096,128]{1,0:T(8,128)(2,1)}, bf16[4096,128]{1,0:T(8,128)(2,1)}, u32[]{:S(2)}, u32[]{:S(2)}) collective-permute-start(bf16[4096,128]{1,0:T(8,128)(2,1)} %refs_0_.1), channel_id=1, source_target_pairs={{0,0},{1,80},{2,16},{3,64},{4,32},{5,112},{6,48},{7,96},{8,1},{9,8... | collective-permute-start | bytes 3145736 | tf_op jit(solution)/shard_map/ppermute | solution.py:225
  11.2 38.8 %collective-permute-start.5 = (bf16[4096,128]{1,0:T(8,128)(2,1)}, bf16[4096,128]{1,0:T(8,128)(2,1)S(1)}, u32[]{:S(2)}, u32[]{:S(2)}) collective-permute-start(bf16[4096,128]{1,0:T(8,128)(2,1)} %refs_0_.1), channel_id=1, source_target_pairs={{0,12},{1,13},{2,14},{3,15},{4,0},{5,1},{6,2},{7,3},{8,4},{9,5},{1... | collective-permute-start | bytes 3145736 | tf_op jit(solution)/shard_map/ppermute | solution.py:225
  15.4 35.9 %collective-permute-start.3 = (bf16[4096,128]{1,0:T(8,128)(2,1)}, bf16[4096,128]{1,0:T(8,128)(2,1)S(1)}, u32[]{:S(2)}, u32[]{:S(2)}) collective-permute-start(bf16[4096,128]{1,0:T(8,128)(2,1)} %refs_0_.1), channel_id=1, source_target_pairs={{0,4},{1,5},{2,6},{3,7},{4,8},{5,9},{6,10},{7,11},{8,12},{9,13},{1... | collective-permute-start | bytes 3145736 | tf_op jit(solution)/shard_map/ppermute | solution.py:225
  28.2 44.2 %collective-permute-start.9 = (bf16[4096,128]{1,0:T(8,128)(2,1)}, bf16[4096,128]{1,0:T(8,128)(2,1)S(1)}, u32[]{:S(2)}, u32[]{:S(2)}) collective-permute-start(bf16[4096,128]{1,0:T(8,128)(2,1)} %collective-permute-done.1.refs_2_), channel_id=1, source_target_pairs={{0,12},{1,13},{2,14},{3,15},{4,0},{5,1},{6,2},{7,3},{8,4},{9,5},{1... | collective-permute-start | bytes 3145736 | tf_op jit(solution)/shard_map/ppermute | solution.py:225
  34.2 43.0 %collective-permute-start.7 = (bf16[4096,128]{1,0:T(8,128)(2,1)}, bf16[4096,128]{1,0:T(8,128)(2,1)}, u32[]{:S(2)}, u32[]{:S(2)}) collective-permute-start(bf16[4096,128]{1,0:T(8,128)(2,1)} %collective-permute-done.1.refs_2_), channel_id=1, source_target_pairs={{0,4},{1,5},{2,6},{3,7},{4,8},{5,9},{6,10},{7,11},{8,12},{9,13},{1... | collective-permute-start | bytes 3145736 | tf_op jit(solution)/shard_map/ppermute | solution.py:225
  40.0 37.3 %collective-permute-start.18 = (bf16[4096,128]{1,0:T(8,128)(2,1)}, bf16[4096,128]{1,0:T(8,128)(2,1)}, u32[]{:S(2)}, u32[]{:S(2)}) collective-permute-start(bf16[4096,128]{1,0:T(8,128)(2,1)} %collective-permute-done.15.refs_16_), channel_id=1, source_target_pairs={{9,105},{11,107},{12,108},{13,109},{14,110},{15,111},{25,121},{27,... | collective-permute-start | bytes 3145736 | tf_op jit(solution)/shard_map/ppermute | solution.py:225
  50.0 87.7 %copy-start = (bf16[4096,128]{1,0:T(8,128)(2,1)}, bf16[4096,128]{1,0:T(8,128)(2,1)S(1)}, u32[]{:S(2)}) copy-start(bf16[4096,128]{1,0:T(8,128)(2,1)S(1)} %collective-permute-done.5.refs_6_) | copy-start | bytes 3145732
  50.0 27.9 %collective-permute-start.17 = (bf16[4096,128]{1,0:T(8,128)(2,1)}, bf16[4096,128]{1,0:T(8,128)(2,1)}, u32[]{:S(2)}, u32[]{:S(2)}) collective-permute-start(bf16[4096,128]{1,0:T(8,128)(2,1)} %collective-permute-done.15.refs_16_), channel_id=1, source_target_pairs={{4,36},{5,37},{6,38},{7,39},{8,40},{9,41},{10,42},{11,43},{12,44},... | collective-permute-start | bytes 3145736 | tf_op jit(solution)/shard_map/ppermute | solution.py:225
  51.3 86.4 %copy-start.1 = (bf16[4096,128]{1,0:T(8,128)(2,1)}, bf16[4096,128]{1,0:T(8,128)(2,1)S(1)}, u32[]{:S(2)}) copy-start(bf16[4096,128]{1,0:T(8,128)(2,1)S(1)} %collective-permute-done.3.refs_4_) | copy-start | bytes 3145732
  51.3 29.1 %collective-permute-start = (bf16[4096,128]{1,0:T(8,128)(2,1)}, bf16[4096,128]{1,0:T(8,128)(2,1)S(1)}, u32[]{:S(2)}, u32[]{:S(2)}) collective-permute-start(bf16[4096,128]{1,0:T(8,128)(2,1)} %refs_0_.1), channel_id=1, source_target_pairs={{0,1},{1,0},{2,3},{3,2},{4,5},{5,4},{6,7},{7,6},{8,9},{9,8},{10,11... | collective-permute-start | bytes 3145736 | tf_op jit(solution)/shard_map/ppermute | solution.py:227
  72.4 65.3 %copy-start.2 = (bf16[4096,128]{1,0:T(8,128)(2,1)}, bf16[4096,128]{1,0:T(8,128)(2,1)S(1)}, u32[]{:S(2)}) copy-start(bf16[4096,128]{1,0:T(8,128)(2,1)S(1)} %collective-permute-done.9.refs_10_) | copy-start | bytes 3145732
  72.5 16.5 %collective-permute-start.11 = (bf16[4096,128]{1,0:T(8,128)(2,1)S(1)}, bf16[4096,128]{1,0:T(8,128)(2,1)S(1)}, u32[]{:S(2)}, u32[]{:S(2)}) collective-permute-start(bf16[4096,128]{1,0:T(8,128)(2,1)S(1)} %broadcast_select_fusion.2), channel_id=1, source_target_pairs={{0,4},{1,13},{2,6},{3,15},{4,8},{5,1},{6,10},{7,3},{8,12},{9,5},{1... | collective-permute-start | bytes 3145736 | tf_op jit(solution)/shard_map/ppermute | solution.py:225
  77.3 13.7 %collective-permute-start.6 = (bf16[4096,128]{1,0:T(8,128)(2,1)S(1)}, bf16[4096,128]{1,0:T(8,128)(2,1)S(1)}, u32[]{:S(2)}, u32[]{:S(2)}) collective-permute-start(bf16[4096,128]{1,0:T(8,128)(2,1)S(1)} %collective-permute-done.5.refs_6_), channel_id=1, source_target_pairs={{0,1},{1,0},{2,3},{3,2},{4,5},{5,4},{6,7},{7,6},{8,9},{9,8},{10,11... | collective-permute-start | bytes 3145736 | tf_op jit(solution)/shard_map/ppermute | solution.py:227
  77.4 13.7 %collective-permute-start.4 = (bf16[4096,128]{1,0:T(8,128)(2,1)S(1)}, bf16[4096,128]{1,0:T(8,128)(2,1)S(1)}, u32[]{:S(2)}, u32[]{:S(2)}) collective-permute-start(bf16[4096,128]{1,0:T(8,128)(2,1)S(1)} %collective-permute-done.3.refs_4_), channel_id=1, source_target_pairs={{0,1},{1,0},{2,3},{3,2},{4,5},{5,4},{6,7},{7,6},{8,9},{9,8},{10,11... | collective-permute-start | bytes 3145736 | tf_op jit(solution)/shard_map/ppermute | solution.py:227
  77.9 16.7 %collective-permute-start.2 = (bf16[4096,128]{1,0:T(8,128)(2,1)}, bf16[4096,128]{1,0:T(8,128)(2,1)S(1)}, u32[]{:S(2)}, u32[]{:S(2)}) collective-permute-start(bf16[4096,128]{1,0:T(8,128)(2,1)} %collective-permute-done.1.refs_2_), channel_id=1, source_target_pairs={{0,1},{1,0},{2,3},{3,2},{4,5},{5,4},{6,7},{7,6},{8,9},{9,8},{10,11... | collective-permute-start | bytes 3145736 | tf_op jit(solution)/shard_map/ppermute | solution.py:227
  80.4 30.5 %copy-start.3 = (bf16[4096,128]{1,0:T(8,128)(2,1)}, bf16[4096,128]{1,0:T(8,128)(2,1)S(1)}, u32[]{:S(2)}) copy-start(bf16[4096,128]{1,0:T(8,128)(2,1)S(1)} %collective-permute-done.refs_1_) | copy-start | bytes 3145732
  80.5 25.7 %collective-permute-start.16 = (bf16[4096,128]{1,0:T(8,128)(2,1)}, bf16[4096,128]{1,0:T(8,128)(2,1)}, u32[]{:S(2)}, u32[]{:S(2)}) collective-permute-start(bf16[4096,128]{1,0:T(8,128)(2,1)} %collective-permute-done.15.refs_16_), channel_id=1, source_target_pairs={{2,18},{3,19},{4,20},{5,21},{6,22},{7,23},{8,24},{9,25},{10,26},{1... | collective-permute-start | bytes 3145736 | tf_op jit(solution)/shard_map/ppermute | solution.py:225
  89.0 22.0 %copy-start.4 = (bf16[4096,128]{1,0:T(8,128)(2,1)}, bf16[4096,128]{1,0:T(8,128)(2,1)S(1)}, u32[]{:S(2)}) copy-start(bf16[4096,128]{1,0:T(8,128)(2,1)S(1)} %collective-permute-done.11.refs_12_) | copy-start | bytes 3145732
  89.0 19.3 %collective-permute-start.12 = (bf16[4096,128]{1,0:T(8,128)(2,1)S(1)}, bf16[4096,128]{1,0:T(8,128)(2,1)S(1)}, u32[]{:S(2)}, u32[]{:S(2)}) collective-permute-start(bf16[4096,128]{1,0:T(8,128)(2,1)S(1)} %collective-permute-done.11.refs_12_), channel_id=1, source_target_pairs={{0,1},{1,0},{2,3},{3,2},{4,5},{5,4},{6,7},{7,6},{8,9},{9,8},{10,11... | collective-permute-start | bytes 3145736 | tf_op jit(solution)/shard_map/ppermute | solution.py:227
  91.0 20.0 %copy-start.5 = (bf16[4096,128]{1,0:T(8,128)(2,1)}, bf16[4096,128]{1,0:T(8,128)(2,1)S(1)}, u32[]{:S(2)}) copy-start(bf16[4096,128]{1,0:T(8,128)(2,1)S(1)} %collective-permute-done.6.refs_7_) | copy-start | bytes 3145732
  91.0 18.6 %collective-permute-start.10 = (bf16[4096,128]{1,0:T(8,128)(2,1)S(1)}, bf16[4096,128]{1,0:T(8,128)(2,1)S(1)}, u32[]{:S(2)}, u32[]{:S(2)}) collective-permute-start(bf16[4096,128]{1,0:T(8,128)(2,1)S(1)} %collective-permute-done.9.refs_10_), channel_id=1, source_target_pairs={{0,1},{1,0},{2,3},{3,2},{4,5},{5,4},{6,7},{7,6},{8,9},{9,8},{10,11... | collective-permute-start | bytes 3145736 | tf_op jit(solution)/shard_map/ppermute | solution.py:227
  91.1 19.9 %copy-start.6 = (bf16[4096,128]{1,0:T(8,128)(2,1)}, bf16[4096,128]{1,0:T(8,128)(2,1)S(1)}, u32[]{:S(2)}) copy-start(bf16[4096,128]{1,0:T(8,128)(2,1)S(1)} %collective-permute-done.4.refs_5_) | copy-start | bytes 3145732
  91.1 19.8 %collective-permute-start.13 = (bf16[4096,128]{1,0:T(8,128)(2,1)S(1)}, bf16[4096,128]{1,0:T(8,128)(2,1)}, u32[]{:S(2)}, u32[]{:S(2)}) collective-permute-start(bf16[4096,128]{1,0:T(8,128)(2,1)S(1)} %broadcast_select_fusion.1), channel_id=1, source_target_pairs={{0,4},{1,13},{2,6},{3,15},{4,8},{5,1},{6,10},{7,3},{8,12},{9,5},{1... | collective-permute-start | bytes 3145736 | tf_op jit(solution)/shard_map/ppermute | solution.py:225
  94.5 16.5 %copy-start.7 = (bf16[4096,128]{1,0:T(8,128)(2,1)}, bf16[4096,128]{1,0:T(8,128)(2,1)S(1)}, u32[]{:S(2)}) copy-start(bf16[4096,128]{1,0:T(8,128)(2,1)S(1)} %collective-permute-done.2.refs_3_) | copy-start | bytes 3145732
  94.6 16.4 %collective-permute-start.21 = (bf16[4096,128]{1,0:T(8,128)(2,1)S(1)}, bf16[4096,128]{1,0:T(8,128)(2,1)}, u32[]{:S(2)}, u32[]{:S(2)}) collective-permute-start(bf16[4096,128]{1,0:T(8,128)(2,1)S(1)} %broadcast_select_fusion), channel_id=1, source_target_pairs={{4,36},{6,38},{8,40},{10,42},{12,44},{13,109},{14,46},{15,111},{20... | collective-permute-start | bytes 3145736 | tf_op jit(solution)/shard_map/ppermute | solution.py:225
  106.2 8.3 %collective-permute-start.8 = (bf16[4096,128]{1,0:T(8,128)(2,1)}, bf16[4096,128]{1,0:T(8,128)(2,1)}, u32[]{:S(2)}, u32[]{:S(2)}) collective-permute-start(bf16[4096,128]{1,0:T(8,128)(2,1)} %collective-permute-done.7.refs_8_), channel_id=1, source_target_pairs={{0,1},{1,0},{2,3},{3,2},{4,5},{5,4},{6,7},{7,6},{8,9},{9,8},{10,11... | collective-permute-start | bytes 3145736 | tf_op jit(solution)/shard_map/ppermute | solution.py:227
  108.2 2.8 %copy-start.8 = (bf16[4096,128]{1,0:T(8,128)(2,1)}, bf16[4096,128]{1,0:T(8,128)(2,1)S(1)}, u32[]{:S(2)}) copy-start(bf16[4096,128]{1,0:T(8,128)(2,1)S(1)} %collective-permute-done.12.refs_13_) | copy-start | bytes 3145732
  108.2 26.9 %collective-permute-start.20 = (bf16[4096,128]{1,0:T(8,128)(2,1)}, bf16[4096,128]{1,0:T(8,128)(2,1)}, u32[]{:S(2)}, u32[]{:S(2)}) collective-permute-start(bf16[4096,128]{1,0:T(8,128)(2,1)} %collective-permute-done.16.refs_17_), channel_id=1, source_target_pairs={{12,108},{13,109},{14,110},{15,111},{30,126},{31,127},{32,0},{33,1... | collective-permute-start | bytes 3145736 | tf_op jit(solution)/shard_map/ppermute | solution.py:225
  109.6 28.1 %collective-permute-start.19 = (bf16[4096,128]{1,0:T(8,128)(2,1)}, bf16[4096,128]{1,0:T(8,128)(2,1)}, u32[]{:S(2)}, u32[]{:S(2)}) collective-permute-start(bf16[4096,128]{1,0:T(8,128)(2,1)} %collective-permute-done.16.refs_17_), channel_id=1, source_target_pairs={{4,36},{5,37},{6,38},{7,39},{8,40},{9,41},{10,42},{11,43},{12,44},... | collective-permute-start | bytes 3145736 | tf_op jit(solution)/shard_map/ppermute | solution.py:225
  110.9 26.8 %collective-permute-start.14 = (bf16[4096,128]{1,0:T(8,128)(2,1)}, bf16[4096,128]{1,0:T(8,128)(2,1)}, u32[]{:S(2)}, u32[]{:S(2)}) collective-permute-start(bf16[4096,128]{1,0:T(8,128)(2,1)} %collective-permute-done.13.refs_14_), channel_id=1, source_target_pairs={{0,1},{1,0},{2,3},{3,2},{4,5},{5,4},{6,7},{7,6},{8,9},{9,8},{10,11... | collective-permute-start | bytes 3145736 | tf_op jit(solution)/shard_map/ppermute | solution.py:227
  111.0 26.6 %collective-permute-start.22 = (bf16[4096,128]{1,0:T(8,128)(2,1)}, bf16[4096,128]{1,0:T(8,128)(2,1)}, u32[]{:S(2)}, u32[]{:S(2)}) collective-permute-start(bf16[4096,128]{1,0:T(8,128)(2,1)} %collective-permute-done.21.refs_22_), channel_id=1, source_target_pairs={{2,18},{3,19},{4,20},{5,21},{6,22},{7,23},{8,24},{9,25},{10,26},{1... | collective-permute-start | bytes 3145736 | tf_op jit(solution)/shard_map/ppermute | solution.py:225
  (1 other events, 1.5 us)

commit v2 on v1

v2 whole, which is shorter than its diff:
```python
import functools

import jax
import jax.numpy as jnp
from jax import lax
from jax.experimental import pallas as pl
from jax.experimental.pallas import tpu as pltpu
from jax.sharding import PartitionSpec as P


ROWS, COLS = 8, 16
BOTH = ("row", "col")


def coords(device):
    row, col = divmod(device, COLS)
    y, x_lo = divmod(row, 2)
    z, rest = divmod(col, 4)
    x_hi, core = divmod(rest, 2)
    return 2 * x_hi + x_lo, y, z, core


def device_at(x, y, z, core):
    x, y, z = x % 4, y % 4, z % 4
    return (y * 2 + x % 2) * COLS + z * 4 + (x // 2) * 2 + core


def moves(step):
    return {d: device_at(*step(*coords(d))) for d in range(ROWS * COLS)}


def transpose_moves():
    out = {}
    for k in range(ROWS):
        z_to, x_hi_to = divmod(k, 2)
        for s in range(COLS):
            z, x_hi, core = s // 4, (s // 2) % 2, s % 2
            shift = (0, 2, 1, 3)[(z % 2) * 2 + core]
            out[k * COLS + s] = device_at(2 * x_hi_to + (x_hi ^ core), z_to + shift, z_to, z // 2)
    return out


HOPS = (
    ("row_b", lambda x, y, z, c: (x + 2, y, z, c), "row_a"),
    ("row_a_1", lambda x, y, z, c: (x, y, z + 1 - 2 * c, c), "row_a"),
    ("row_a_2", lambda x, y, z, c: (x, y, z - 1 + 2 * c, c), "row_a"),
    ("row_b_1", lambda x, y, z, c: (x, y, z + 1 - 2 * c, c), "row_b"),
    ("row_b_2", lambda x, y, z, c: (x, y, z - 1 + 2 * c, c), "row_b"),
    ("row_a_far", lambda x, y, z, c: (x, y, z + 1 - 2 * c, c), "row_a_1"),
    ("row_b_far", lambda x, y, z, c: (x, y, z + 1 - 2 * c, c), "row_b_1"),
    ("col_a", None, "row_a"),
    ("col_b", lambda x, y, z, c: (x ^ 1, y, z, c), "col_a"),
    ("col_a_1", lambda x, y, z, c: (x, y + 1 - 2 * c, z, c), "col_a"),
    ("col_a_2", lambda x, y, z, c: (x, y - 1 + 2 * c, z, c), "col_a"),
    ("col_b_1", lambda x, y, z, c: (x, y + 1 - 2 * c, z, c), "col_b"),
    ("col_b_2", lambda x, y, z, c: (x, y - 1 + 2 * c, z, c), "col_b"),
    ("col_a_far", lambda x, y, z, c: (x, y + 1 - 2 * c, z, c), "col_a_1"),
    ("col_b_far", lambda x, y, z, c: (x ^ 1, y, z, c), "col_a_far"),
)
ROW_NAMES = ("row_a", "row_b", "row_a_1", "row_a_2", "row_b_1", "row_b_2", "row_a_far", "row_b_far")
COL_NAMES = ("col_a", "col_b", "col_a_1", "col_a_2", "col_b_1", "col_b_2", "col_a_far", "col_b_far")
OTHER_CORE = sorted(moves(lambda x, y, z, c: (x, y, z, 1 - c)).items())


def hop_shift(name, core):
    return {"1": 2 * core - 1, "2": 1 - 2 * core, "far": 2}.get(name.split("_")[-1], 0)


def row_place(name, col, other):
    core = (col & 1) ^ other
    z = ((col >> 2) + hop_shift(name, core)) & 3
    return z * 4 + (((col >> 1) & 1) ^ (1 if "_b" in name else 0)) * 2 + core


def col_place(name, row, col):
    shift = ((row >> 1) + hop_shift(name, col & 1) - (col >> 2)) & 3
    core, z = shift >> 1, shift & 1
    return z * 4 + ((row & 1) ^ (1 if "_b" in name else 0) ^ core) * 2 + core


def active(row, col):
    return col // 2 >= row


@functools.cache
def plan():
    devices = range(ROWS * COLS)
    full = {n: transpose_moves() if step is None else moves(step) for n, step, _ in HOPS}
    holds = {"row_a": {d: d for d in devices}}
    for name, _, sent in HOPS:
        holds[name] = {t: holds[sent][s] for s, t in full[name].items()}
    needed = {n: set() for n in holds}
    for d in devices:
        row, col = divmod(d, COLS)
        for n in ROW_NAMES:
            for other in (0, 1):
                assert holds[n][d ^ other] == row * COLS + row_place(n, col, other)
        for n in COL_NAMES:
            assert holds[n][d] == col // 2 * COLS + col % 2 * 8 + col_place(n, row, col)
        if active(row, col):
            for n in ROW_NAMES:
                needed[n] |= {d, d ^ 1}
            for n in COL_NAMES:
                needed[n].add(d)
    pairs = {}
    for name, _, sent in reversed(HOPS):
        pairs[name] = sorted((s, t) for s, t in full[name].items() if t in needed[name])
        needed[sent] |= {s for s, _ in pairs[name]}
    return pairs


def tile_kernel(row_names, col_names, group, *refs):
    n_left, n_right = 2 * len(row_names), len(col_names)
    left, right = refs[:n_left], refs[n_left : n_left + n_right]
    out, left_buf, right_buf, stage, left_at, left_sem, right_sem, out_sem = refs[-8:]
    n_steps = n_left // group
    row, col = lax.axis_index("row"), lax.axis_index("col")
    is_active = active(row, col)
    row0, col0 = row * out.shape[0], col * out.shape[1]
    for i in range(n_left):
        left_at[i] = row_place(row_names[i // 2], col, i % 2)
    right_at = [col_place(n, row, col) for n in col_names]

    def left_copy(i):
        return pltpu.make_async_copy(
            left[i], left_buf.at[i // group, :, pl.ds(i % group * 128, 128)], left_sem.at[i]
        )

    def right_copy(j):
        return pltpu.make_async_copy(right[j], right_buf.at[:, pl.ds(j * 128, 128)], right_sem.at[j])

    def out_copy(slot, i, part, j):
        place = left_at[group * i + part]
        return pltpu.make_async_copy(
            stage.at[slot, pl.ds(part * 128, 128), pl.ds(j * 128, 128)],
            out.at[
                pl.ds(pl.multiple_of(place * 128, 128), 128),
                pl.ds(pl.multiple_of(right_at[j] * 128, 128), 128),
            ],
            out_sem.at[slot, part, j],
        )

    def each_out(slot, i, act):
        for part in range(group):
            for j in range(n_right):
                act(out_copy(slot, i, part, j))

    @pl.when(is_active)
    def _():
        for j in range(n_right):
            right_copy(j).start()
        for i in range(group):
            left_copy(i).start()
        for j in range(n_right):
            right_copy(j).wait()

    @pl.when(jnp.logical_not(is_active))
    def _():
        stage[...] = jnp.zeros_like(stage)

    @pl.loop(0, n_steps)
    def _(i):
        slot = i % 2

        @pl.when(i >= 2)
        def _():
            each_out(slot, i - 2, lambda c: c.wait())

        for step in range(1, n_steps):

            @pl.when(is_active & (i + 1 == step))
            def _():
                for part in range(group):
                    left_copy(step * group + part).start()

        @pl.when(is_active)
        def _():
            for part in range(group):
                pltpu.make_async_copy(
                    left[0], left_buf.at[i, :, pl.ds(part * 128, 128)], left_sem.at[group * i + part]
                ).wait()
            product = lax.dot_general(
                left_buf[i], right_buf[...], (((0,), (0,)), ((), ())), preferred_element_type=jnp.float32
            )
            ahead = lax.broadcasted_iota(jnp.int32, (128, 128), 1) - lax.broadcasted_iota(jnp.int32, (128, 128), 0)
            for part in range(group):
                for j in range(n_right):
                    lag = row0 + left_at[group * i + part] * 128 - col0 - right_at[j] * 128
                    block = product[part * 128 : part * 128 + 128, j * 128 : j * 128 + 128]
                    stage[slot, part * 128 : part * 128 + 128, j * 128 : j * 128 + 128] = jnp.where(
                        ahead >= lag, block, 0.0
                    )

        each_out(slot, i, lambda c: c.start())

    for i in range(max(n_steps - 2, 0), n_steps):
        each_out(i % 2, i, lambda c: c.wait())


def tile_part(row_names, col_names, held, shape, previous=None):
    left = [h for n in row_names for h in (held[n], held["other_" + n])]
    right = [held[n] for n in col_names]
    n_left, n_right = len(left), len(right)
    group = max(g for g in range(1, n_left + 1) if n_left % g == 0 and g * n_right <= 16)
    any_spec = pl.BlockSpec(memory_space=pl.ANY)
    extra = () if previous is None else (previous,)

    def kernel(*refs):
        if extra:
            refs = refs[: n_left + n_right] + refs[n_left + n_right + 1 :]
        tile_kernel(row_names, col_names, group, *refs)

    return pl.pallas_call(
        kernel,
        out_shape=jax.ShapeDtypeStruct(shape, jnp.float32),
        in_specs=[any_spec] * (n_left + n_right + len(extra)),
        out_specs=any_spec,
        scratch_shapes=[
            pltpu.VMEM((n_left // group, 4096, 128 * group), jnp.bfloat16),
            pltpu.VMEM((4096, 128 * n_right), jnp.bfloat16),
            pltpu.VMEM((2, 128 * group, 128 * n_right), jnp.float32),
            pltpu.SMEM((n_left,), jnp.int32),
            pltpu.SemaphoreType.DMA((n_left,)),
            pltpu.SemaphoreType.DMA((n_right,)),
            pltpu.SemaphoreType.DMA((2, group, n_right)),
        ],
        input_output_aliases={n_left + n_right: 0} if extra else {},
        compiler_params=pltpu.CompilerParams(vmem_limit_bytes=67043328),
        cost_estimate=pl.CostEstimate(
            flops=2 * 4096 * 128 * 128 * n_left * n_right,
            bytes_accessed=(n_left + n_right) * 4096 * 128 * 2 + n_left * n_right * 128 * 128 * 4,
            transcendentals=0,
        ),
    )(*left, *right, *extra)


def shards(filtered_bands):
    pairs = plan()
    shape = (filtered_bands.shape[1] * COLS, filtered_bands.shape[1] * ROWS)
    held = {"row_a": filtered_bands}
    for name, _, sent in HOPS:
        held[name] = lax.ppermute(held[sent], BOTH, pairs[name])
    for name in ROW_NAMES:
        held["other_" + name] = lax.ppermute(held[name], BOTH, OTHER_CORE)
    out = None
    for (row_names, col_names) in TILES.values():
        out = tile_part(row_names, col_names, held, shape, out)
    return out


TILES = {
    "tile_1": (("row_a", "row_b", "row_a_1", "row_a_2"), ("col_a", "col_b", "col_a_1", "col_a_2")),
    "tile_2": (("row_a_far", "row_b_1", "row_b_2", "row_b_far"), ("col_a", "col_b", "col_a_1", "col_a_2")),
    "tile_3": (ROW_NAMES, ("col_b_1", "col_b_2", "col_a_far", "col_b_far")),
}


def solution(mesh):
    return jax.shard_map(
        shards,
        mesh=mesh,
        in_specs=(P(None, ("row", "col")),),
        out_specs=P("row", "col"),
        check_vma=False,
    )
```

time: 170 us -> 164 us (0.965); the launches traced: 167 us -> 163 us
  starting transfers between devices: 54 us -> 48.8 us
  Pallas kernels: 29.5 us -> 33.7 us
  other arithmetic: 2.24 us -> 0 us
    ppermute x15, starting transfers between devices: 42.5 us -> 35.7 us  [shards(): held[name] = lax.ppermute(held[sent], BOTH, pairs[name])]
    pallas_call x1 -> x3, Pallas kernels: 29.5 us -> 33.7 us  [tile_part(): pl.pallas_call(kernel, out_shape=jax.ShapeDtypeStruct(shape, jnp.float32)...]
  transfers between devices with their start and end apart: 23 -> 23, of which waited for: 8 -> 8; matrix products, arithmetic and copies ran while one was open for 2% -> 0% of each run, Pallas kernels for 0% -> 12%
where the time goes in v2:
time: 164 us; the launch traced here: 163 us
  waiting for transfers between devices  80 us (49%)
  starting transfers between devices  48.8 us (30%)
  Pallas kernels  33.7 us (21%)
    ppermute x15, waiting for transfers between devices, shards(): held[name] = lax.ppermute(held[sent], BOTH, pairs[name])  80 us
    ppermute x15, starting transfers between devices, shards(): held[name] = lax.ppermute(held[sent], BOTH, pairs[name])  35.7 us
    pallas_call x3, Pallas kernels, tile_part(): pl.pallas_call(kernel, out_shape=jax.ShapeDtypeStruct(shape, jnp.float32)...  33.7 us
    ppermute x8, starting transfers between devices, shards(): held['other_' + name] = lax.ppermute(held[name], BOTH, OTHER_CORE)  13 us
  transfers between devices with their start and end apart: 23, of which 8 were waited for; matrix products, arithmetic and copies ran while one was open for 0% of the time, Pallas kernels for 12%

profile of v2, /device:TPU:1, one launch (start us, length us, event | category | flops | bytes accessed | tf_op | source)
XLA Modules:
  0.0 162.9 jit_solution(3006990042257465692)
XLA Ops:
  0.0 7.1 %collective-permute-start.15 = (bf16[4096,128]{1,0:T(8,128)(2,1)}, bf16[4096,128]{1,0:T(8,128)(2,1)S(1)}, u32[]{:S(2)}, u32[]{:S(2)}) collective-permute-start(bf16[4096,128]{1,0:T(8,128)(2,1)} %refs_0_.3), channel_id=1, source_target_pairs={{0,0},{1,80},{2,16},{3,64},{4,32},{5,112},{6,48},{7,96},{8,1},{9,8... | collective-permute-start | bytes 3145736 | tf_op jit(solution)/shard_map/ppermute | solution.py:242
  7.1 3.7 %collective-permute-start.1 = (bf16[4096,128]{1,0:T(8,128)(2,1)}, bf16[4096,128]{1,0:T(8,128)(2,1)S(1)}, u32[]{:S(2)}, u32[]{:S(2)}) collective-permute-start(bf16[4096,128]{1,0:T(8,128)(2,1)} %refs_0_.3), channel_id=1, source_target_pairs={{0,2},{1,3},{2,0},{3,1},{4,6},{5,7},{6,4},{7,5},{8,10},{9,11},{10,... | collective-permute-start | bytes 3145736 | tf_op jit(solution)/shard_map/ppermute | solution.py:242
  10.8 3.6 %collective-permute-start.3 = (bf16[4096,128]{1,0:T(8,128)(2,1)}, bf16[4096,128]{1,0:T(8,128)(2,1)S(1)}, u32[]{:S(2)}, u32[]{:S(2)}) collective-permute-start(bf16[4096,128]{1,0:T(8,128)(2,1)} %refs_0_.3), channel_id=1, source_target_pairs={{0,4},{1,13},{2,6},{3,15},{4,8},{5,1},{6,10},{7,3},{8,12},{9,5},{1... | collective-permute-start | bytes 3145736 | tf_op jit(solution)/shard_map/ppermute | solution.py:242
  14.4 1.9 %collective-permute-start.5 = (bf16[4096,128]{1,0:T(8,128)(2,1)}, bf16[4096,128]{1,0:T(8,128)(2,1)S(1)}, u32[]{:S(2)}, u32[]{:S(2)}) collective-permute-start(bf16[4096,128]{1,0:T(8,128)(2,1)} %refs_0_.3), channel_id=1, source_target_pairs={{0,12},{1,5},{2,14},{3,7},{4,0},{5,9},{6,2},{7,11},{8,4},{9,13},{1... | collective-permute-start | bytes 3145736 | tf_op jit(solution)/shard_map/ppermute | solution.py:242
  16.3 0.1 collective-permute-start
  16.4 12.1 %collective-permute-done.15.refs_8_ = bf16[4096,128]{1,0:T(8,128)(2,1)S(1)} collective-permute-done((bf16[4096,128]{1,0:T(8,128)(2,1)}, bf16[4096,128]{1,0:T(8,128)(2,1)S(1)}, u32[]{:S(2)}, u32[]{:S(2)}) %collective-permute-start.15) | collective-permute-done | bytes 1048608 | tf_op jit(solution)/shard_map/ppermute | solution.py:242
  28.5 1.3 collective-permute-start.16
  29.8 25.1 %collective-permute-done.1.refs_2_ = bf16[4096,128]{1,0:T(8,128)(2,1)S(1)} collective-permute-done((bf16[4096,128]{1,0:T(8,128)(2,1)}, bf16[4096,128]{1,0:T(8,128)(2,1)S(1)}, u32[]{:S(2)}, u32[]{:S(2)}) %collective-permute-start.1) | collective-permute-done | bytes 1048608 | tf_op jit(solution)/shard_map/ppermute | solution.py:242
  54.9 1.3 collective-permute-start.19
  56.2 0.1 collective-permute-start.2
  56.3 1.3 collective-permute-start.22
  57.6 2.0 %collective-permute-start.7 = (bf16[4096,128]{1,0:T(8,128)(2,1)S(1)}, bf16[4096,128]{1,0:T(8,128)(2,1)S(1)}, u32[]{:S(2)}, u32[]{:S(2)}) collective-permute-start(bf16[4096,128]{1,0:T(8,128)(2,1)S(1)} %collective-permute-done.1.refs_2_), channel_id=1, source_target_pairs={{0,4},{1,13},{2,6},{3,15},{4,8},{5,1},{6,10},{7,3},{8,12},{9,5},{1... | collective-permute-start | bytes 3145736 | tf_op jit(solution)/shard_map/ppermute | solution.py:242
  59.6 6.8 %collective-permute-done.16.refs_9_ = bf16[4096,128]{1,0:T(8,128)(2,1)} collective-permute-done((bf16[4096,128]{1,0:T(8,128)(2,1)S(1)}, bf16[4096,128]{1,0:T(8,128)(2,1)}, u32[]{:S(2)}, u32[]{:S(2)}) %collective-permute-start.16) | collective-permute-done | bytes 1048608 | tf_op jit(solution)/shard_map/ppermute | solution.py:242
  66.4 13.2 %collective-permute-done.19.refs_10_ = bf16[4096,128]{1,0:T(8,128)(2,1)S(1)} collective-permute-done((bf16[4096,128]{1,0:T(8,128)(2,1)S(1)}, bf16[4096,128]{1,0:T(8,128)(2,1)S(1)}, u32[]{:S(2)}, u32[]{:S(2)}) %collective-permute-start.19) | collective-permute-done | bytes 1048608 | tf_op jit(solution)/shard_map/ppermute | solution.py:242
  79.6 1.9 %collective-permute-start.9 = (bf16[4096,128]{1,0:T(8,128)(2,1)S(1)}, bf16[4096,128]{1,0:T(8,128)(2,1)S(1)}, u32[]{:S(2)}, u32[]{:S(2)}) collective-permute-start(bf16[4096,128]{1,0:T(8,128)(2,1)S(1)} %collective-permute-done.1.refs_2_), channel_id=1, source_target_pairs={{0,12},{1,5},{2,14},{3,7},{4,0},{5,9},{6,2},{7,11},{8,4},{9,13},{1... | collective-permute-start | bytes 3145736 | tf_op jit(solution)/shard_map/ppermute | solution.py:242
  81.5 0.1 collective-permute-start.6
  81.6 4.6 %collective-permute-start.11 = (bf16[4096,128]{1,0:T(8,128)(2,1)S(1)}, bf16[4096,128]{1,0:T(8,128)(2,1)}, u32[]{:S(2)}, u32[]{:S(2)}) collective-permute-start(bf16[4096,128]{1,0:T(8,128)(2,1)S(1)} %collective-permute-done.3.refs_4_), channel_id=1, source_target_pairs={{0,4},{1,13},{2,6},{3,15},{4,8},{5,1},{6,10},{7,3},{8,12},{9,5},{1... | collective-permute-start | bytes 3145736 | tf_op jit(solution)/shard_map/ppermute | solution.py:242
  86.2 1.9 %collective-permute-start.13 = (bf16[4096,128]{1,0:T(8,128)(2,1)S(1)}, bf16[4096,128]{1,0:T(8,128)(2,1)}, u32[]{:S(2)}, u32[]{:S(2)}) collective-permute-start(bf16[4096,128]{1,0:T(8,128)(2,1)S(1)} %collective-permute-done.7.refs_2_.refs_8_), channel_id=1, source_target_pairs={{0,4},{1,13},{2,6},{3,15},{4,8},{5,1},{6,10},{7,3},{8,12},{9,5},{1... | collective-permute-start | bytes 3145736 | tf_op jit(solution)/shard_map/ppermute | solution.py:242
  88.2 0.1 collective-permute-start.8
  88.3 16.5 %collective-permute-done.9.refs_4_.refs_10_ = bf16[4096,128]{1,0:T(8,128)(2,1)S(1)} collective-permute-done((bf16[4096,128]{1,0:T(8,128)(2,1)S(1)}, bf16[4096,128]{1,0:T(8,128)(2,1)S(1)}, u32[]{:S(2)}, u32[]{:S(2)}) %collective-permute-start.9) | collective-permute-done | bytes 1048608 | tf_op jit(solution)/shard_map/ppermute | solution.py:242
  104.7 1.3 collective-permute-start.20
  106.1 2.3 %collective-permute-start.12 = (bf16[4096,128]{1,0:T(8,128)(2,1)}, bf16[4096,128]{1,0:T(8,128)(2,1)}, u32[]{:S(2)}, u32[]{:S(2)}) collective-permute-start(bf16[4096,128]{1,0:T(8,128)(2,1)} %collective-permute-done.11.refs_0_.refs_12_), channel_id=1, source_target_pairs={{0,1},{1,0},{2,3},{3,2},{4,5},{5,4},{6,7},{7,6},{8,9},{9,8},{10,11... | collective-permute-start | bytes 3145736 | tf_op jit(solution)/shard_map/ppermute | solution.py:244
  108.3 0.8 collective-permute-done.13.refs_6_.refs_14_
  109.2 10.4 %collective-permute-start.14 = (bf16[4096,128]{1,0:T(8,128)(2,1)}, bf16[4096,128]{1,0:T(8,128)(2,1)}, u32[]{:S(2)}, u32[]{:S(2)}) collective-permute-start(bf16[4096,128]{1,0:T(8,128)(2,1)} %collective-permute-done.13.refs_6_.refs_14_), channel_id=1, source_target_pairs={{0,1},{1,0},{2,3},{3,2},{4,5},{5,4},{6,7},{7,6},{8,9},{9,8},{10,11... | collective-permute-start | bytes 3145736 | tf_op jit(solution)/shard_map/ppermute | solution.py:244
  119.6 1.3 collective-permute-start.17
  120.9 1.3 collective-permute-start.18
  122.3 1.3 collective-permute-start.21
  123.6 9.6 %shard_map.17.refs_12_ = f32[2048,1024]{1,0:T(8,128)} custom-call(bf16[4096,128]{1,0:T(8,128)(2,1)} %refs_0_.3, bf16[4096,128]{1,0:T(8,128)(2,1)} %copy-done.3, bf16[4096,128]{1,0:T(8,128)(2,1)} %copy-done, bf16[4096,128]{1,0:T(8,128)(2,1)} %copy-done.5, bf16[4096,128]{1,0:T(8,128)(2,1)} %copy-done.1, bf16[4096,128]{1,0:T(8,128)(2,1)} %copy-done.8, ...), custom_call_target="tpu_custom_call" | custom-call | flops 4294967296 | bytes 14680064 | tf_op jit(solution)/shard_map/pallas_call | solution.py:213
  133.2 9.6 %shard_map.18.refs_20_ = f32[2048,1024]{1,0:T(8,128)} custom-call(bf16[4096,128]{1,0:T(8,128)(2,1)} %collective-permute-done.11.refs_0_.refs_12_, bf16[4096,128]{1,0:T(8,128)(2,1)} %collective-permute-done.12.refs_1_.refs_13_, bf16[4096,128]{1,0:T(8,128)(2,1)} %copy-done.7, bf16[4096,128]{1,0:T(8,128)(2,1)} %copy-done.12, ...), custom_call_target="tpu_custom_call", output_to_operand_aliasing={{}: (12, {})} | custom-call | flops 4294967296 | bytes 14680064 | tf_op jit(solution)/shard_map/pallas_call | solution.py:213
  142.8 2.4 %collective-permute-done.17.refs_16_ = bf16[4096,128]{1,0:T(8,128)(2,1)} collective-permute-done((bf16[4096,128]{1,0:T(8,128)(2,1)}, bf16[4096,128]{1,0:T(8,128)(2,1)}, u32[]{:S(2)}, u32[]{:S(2)}) %collective-permute-start.17) | collective-permute-done | bytes 1048608 | tf_op jit(solution)/shard_map/ppermute | solution.py:242
  145.2 3.2 %collective-permute-done.18.refs_17_ = bf16[4096,128]{1,0:T(8,128)(2,1)} collective-permute-done((bf16[4096,128]{1,0:T(8,128)(2,1)}, bf16[4096,128]{1,0:T(8,128)(2,1)}, u32[]{:S(2)}, u32[]{:S(2)}) %collective-permute-start.18) | collective-permute-done | bytes 1048608 | tf_op jit(solution)/shard_map/ppermute | solution.py:242
  148.4 14.5 %shard_map.19 = f32[2048,1024]{1,0:T(8,128)} custom-call(bf16[4096,128]{1,0:T(8,128)(2,1)} %refs_0_.3, bf16[4096,128]{1,0:T(8,128)(2,1)} %copy-done.3, bf16[4096,128]{1,0:T(8,128)(2,1)} %copy-done, bf16[4096,128]{1,0:T(8,128)(2,1)} %copy-done.5, bf16[4096,128]{1,0:T(8,128)(2,1)} %copy-done.1, ...), custom_call_target="tpu_custom_call", output_to_operand_aliasing={{}: (20, {})} | custom-call | flops 8589934592 | bytes 25165824 | tf_op jit(solution)/shard_map/pallas_call | solution.py:213
  (45 shorter events, 0.1 us)
Async XLA Ops:
  0.0 28.5 %collective-permute-start.15 = (bf16[4096,128]{1,0:T(8,128)(2,1)}, bf16[4096,128]{1,0:T(8,128)(2,1)S(1)}, u32[]{:S(2)}, u32[]{:S(2)}) collective-permute-start(bf16[4096,128]{1,0:T(8,128)(2,1)} %refs_0_.3), channel_id=1, source_target_pairs={{0,0},{1,80},{2,16},{3,64},{4,32},{5,112},{6,48},{7,96},{8,1},{9,8... | collective-permute-start | bytes 3145736 | tf_op jit(solution)/shard_map/ppermute | solution.py:242
  7.1 47.7 %collective-permute-start.1 = (bf16[4096,128]{1,0:T(8,128)(2,1)}, bf16[4096,128]{1,0:T(8,128)(2,1)S(1)}, u32[]{:S(2)}, u32[]{:S(2)}) collective-permute-start(bf16[4096,128]{1,0:T(8,128)(2,1)} %refs_0_.3), channel_id=1, source_target_pairs={{0,2},{1,3},{2,0},{3,1},{4,6},{5,7},{6,4},{7,5},{8,10},{9,11},{10,... | collective-permute-start | bytes 3145736 | tf_op jit(solution)/shard_map/ppermute | solution.py:242
  10.8 45.4 %collective-permute-start.3 = (bf16[4096,128]{1,0:T(8,128)(2,1)}, bf16[4096,128]{1,0:T(8,128)(2,1)S(1)}, u32[]{:S(2)}, u32[]{:S(2)}) collective-permute-start(bf16[4096,128]{1,0:T(8,128)(2,1)} %refs_0_.3), channel_id=1, source_target_pairs={{0,4},{1,13},{2,6},{3,15},{4,8},{5,1},{6,10},{7,3},{8,12},{9,5},{1... | collective-permute-start | bytes 3145736 | tf_op jit(solution)/shard_map/ppermute | solution.py:242
  14.4 41.9 %collective-permute-start.5 = (bf16[4096,128]{1,0:T(8,128)(2,1)}, bf16[4096,128]{1,0:T(8,128)(2,1)S(1)}, u32[]{:S(2)}, u32[]{:S(2)}) collective-permute-start(bf16[4096,128]{1,0:T(8,128)(2,1)} %refs_0_.3), channel_id=1, source_target_pairs={{0,12},{1,5},{2,14},{3,7},{4,0},{5,9},{6,2},{7,11},{8,4},{9,13},{1... | collective-permute-start | bytes 3145736 | tf_op jit(solution)/shard_map/ppermute | solution.py:242
  16.3 41.3 %collective-permute-start = (bf16[4096,128]{1,0:T(8,128)(2,1)}, bf16[4096,128]{1,0:T(8,128)(2,1)S(1)}, u32[]{:S(2)}, u32[]{:S(2)}) collective-permute-start(bf16[4096,128]{1,0:T(8,128)(2,1)} %refs_0_.3), channel_id=1, source_target_pairs={{0,1},{1,0},{2,3},{3,2},{4,5},{5,4},{6,7},{7,6},{8,9},{9,8},{10,11... | collective-permute-start | bytes 3145736 | tf_op jit(solution)/shard_map/ppermute | solution.py:244
  28.5 80.7 %copy-start.4 = (bf16[4096,128]{1,0:T(8,128)(2,1)}, bf16[4096,128]{1,0:T(8,128)(2,1)S(1)}, u32[]{:S(2)}) copy-start(bf16[4096,128]{1,0:T(8,128)(2,1)S(1)} %collective-permute-done.15.refs_8_) | copy-start | bytes 3145732
  28.5 37.9 %collective-permute-start.16 = (bf16[4096,128]{1,0:T(8,128)(2,1)S(1)}, bf16[4096,128]{1,0:T(8,128)(2,1)}, u32[]{:S(2)}, u32[]{:S(2)}) collective-permute-start(bf16[4096,128]{1,0:T(8,128)(2,1)S(1)} %collective-permute-done.15.refs_8_), channel_id=1, source_target_pairs={{2,18},{3,19},{4,20},{5,21},{6,22},{7,23},{8,24},{9,25},{10,26},{1... | collective-permute-start | bytes 3145736 | tf_op jit(solution)/shard_map/ppermute | solution.py:242
  54.9 24.7 %collective-permute-start.19 = (bf16[4096,128]{1,0:T(8,128)(2,1)S(1)}, bf16[4096,128]{1,0:T(8,128)(2,1)S(1)}, u32[]{:S(2)}, u32[]{:S(2)}) collective-permute-start(bf16[4096,128]{1,0:T(8,128)(2,1)S(1)} %collective-permute-done.15.refs_8_), channel_id=1, source_target_pairs={{4,36},{6,38},{8,40},{9,105},{10,42},{11,107},{12,44},{13,109},{14... | collective-permute-start | bytes 3145736 | tf_op jit(solution)/shard_map/ppermute | solution.py:242
  56.2 48.6 %copy-start.1 = (bf16[4096,128]{1,0:T(8,128)(2,1)}, bf16[4096,128]{1,0:T(8,128)(2,1)S(1)}, u32[]{:S(2)}) copy-start(bf16[4096,128]{1,0:T(8,128)(2,1)S(1)} %collective-permute-done.3.refs_4_) | copy-start | bytes 3145732
  56.2 25.3 %collective-permute-start.2 = (bf16[4096,128]{1,0:T(8,128)(2,1)S(1)}, bf16[4096,128]{1,0:T(8,128)(2,1)S(1)}, u32[]{:S(2)}, u32[]{:S(2)}) collective-permute-start(bf16[4096,128]{1,0:T(8,128)(2,1)S(1)} %collective-permute-done.1.refs_2_), channel_id=1, source_target_pairs={{0,1},{1,0},{2,3},{3,2},{4,5},{5,4},{6,7},{7,6},{8,9},{9,8},{10,11... | collective-permute-start | bytes 3145736 | tf_op jit(solution)/shard_map/ppermute | solution.py:244
  56.3 49.8 %copy-start.2 = (bf16[4096,128]{1,0:T(8,128)(2,1)}, bf16[4096,128]{1,0:T(8,128)(2,1)S(1)}, u32[]{:S(2)}) copy-start(bf16[4096,128]{1,0:T(8,128)(2,1)S(1)} %collective-permute-done.5.refs_6_) | copy-start | bytes 3145732
  56.3 25.3 %collective-permute-start.22 = (bf16[4096,128]{1,0:T(8,128)(2,1)S(1)}, bf16[4096,128]{1,0:T(8,128)(2,1)S(1)}, u32[]{:S(2)}, u32[]{:S(2)}) collective-permute-start(bf16[4096,128]{1,0:T(8,128)(2,1)S(1)} %collective-permute-done.15.refs_8_), channel_id=1, source_target_pairs={{5,37},{7,39},{9,41},{11,43},{12,108},{13,45},{14,110},{15,47},{23... | collective-permute-start | bytes 3145736 | tf_op jit(solution)/shard_map/ppermute | solution.py:242
  57.6 50.7 %copy-start.3 = (bf16[4096,128]{1,0:T(8,128)(2,1)}, bf16[4096,128]{1,0:T(8,128)(2,1)S(1)}, u32[]{:S(2)}) copy-start(bf16[4096,128]{1,0:T(8,128)(2,1)S(1)} %collective-permute-done.refs_1_) | copy-start | bytes 3145732
  57.6 28.6 %collective-permute-start.7 = (bf16[4096,128]{1,0:T(8,128)(2,1)S(1)}, bf16[4096,128]{1,0:T(8,128)(2,1)S(1)}, u32[]{:S(2)}, u32[]{:S(2)}) collective-permute-start(bf16[4096,128]{1,0:T(8,128)(2,1)S(1)} %collective-permute-done.1.refs_2_), channel_id=1, source_target_pairs={{0,4},{1,13},{2,6},{3,15},{4,8},{5,1},{6,10},{7,3},{8,12},{9,5},{1... | collective-permute-start | bytes 3145736 | tf_op jit(solution)/shard_map/ppermute | solution.py:242
  66.4 21.8 %collective-permute-start.4 = (bf16[4096,128]{1,0:T(8,128)(2,1)S(1)}, bf16[4096,128]{1,0:T(8,128)(2,1)S(1)}, u32[]{:S(2)}, u32[]{:S(2)}) collective-permute-start(bf16[4096,128]{1,0:T(8,128)(2,1)S(1)} %collective-permute-done.3.refs_4_), channel_id=1, source_target_pairs={{0,1},{1,0},{2,3},{3,2},{4,5},{5,4},{6,7},{7,6},{8,9},{9,8},{10,11... | collective-permute-start | bytes 3145736 | tf_op jit(solution)/shard_map/ppermute | solution.py:244
  79.6 40.0 %copy-start.6 = (bf16[4096,128]{1,0:T(8,128)(2,1)}, bf16[4096,128]{1,0:T(8,128)(2,1)S(1)}, u32[]{:S(2)}) copy-start(bf16[4096,128]{1,0:T(8,128)(2,1)S(1)} %collective-permute-done.19.refs_10_) | copy-start | bytes 3145732
  79.6 25.2 %collective-permute-start.9 = (bf16[4096,128]{1,0:T(8,128)(2,1)S(1)}, bf16[4096,128]{1,0:T(8,128)(2,1)S(1)}, u32[]{:S(2)}, u32[]{:S(2)}) collective-permute-start(bf16[4096,128]{1,0:T(8,128)(2,1)S(1)} %collective-permute-done.1.refs_2_), channel_id=1, source_target_pairs={{0,12},{1,5},{2,14},{3,7},{4,0},{5,9},{6,2},{7,11},{8,4},{9,13},{1... | collective-permute-start | bytes 3145736 | tf_op jit(solution)/shard_map/ppermute | solution.py:242
  81.5 38.1 %copy-start.5 = (bf16[4096,128]{1,0:T(8,128)(2,1)}, bf16[4096,128]{1,0:T(8,128)(2,1)S(1)}, u32[]{:S(2)}) copy-start(bf16[4096,128]{1,0:T(8,128)(2,1)S(1)} %collective-permute-done.2.refs_3_) | copy-start | bytes 3145732
  81.5 23.2 %collective-permute-start.6 = (bf16[4096,128]{1,0:T(8,128)(2,1)S(1)}, bf16[4096,128]{1,0:T(8,128)(2,1)S(1)}, u32[]{:S(2)}, u32[]{:S(2)}) collective-permute-start(bf16[4096,128]{1,0:T(8,128)(2,1)S(1)} %collective-permute-done.5.refs_6_), channel_id=1, source_target_pairs={{0,1},{1,0},{2,3},{3,2},{4,5},{5,4},{6,7},{7,6},{8,9},{9,8},{10,11... | collective-permute-start | bytes 3145736 | tf_op jit(solution)/shard_map/ppermute | solution.py:244
  81.6 40.6 %copy-start.9 = (bf16[4096,128]{1,0:T(8,128)(2,1)}, bf16[4096,128]{1,0:T(8,128)(2,1)S(1)}, u32[]{:S(2)}) copy-start(bf16[4096,128]{1,0:T(8,128)(2,1)S(1)} %collective-permute-done.22.refs_11_) | copy-start | bytes 3145732
  81.6 24.4 %collective-permute-start.11 = (bf16[4096,128]{1,0:T(8,128)(2,1)S(1)}, bf16[4096,128]{1,0:T(8,128)(2,1)}, u32[]{:S(2)}, u32[]{:S(2)}) collective-permute-start(bf16[4096,128]{1,0:T(8,128)(2,1)S(1)} %collective-permute-done.3.refs_4_), channel_id=1, source_target_pairs={{0,4},{1,13},{2,6},{3,15},{4,8},{5,1},{6,10},{7,3},{8,12},{9,5},{1... | collective-permute-start | bytes 3145736 | tf_op jit(solution)/shard_map/ppermute | solution.py:242
  86.2 36.0 %copy-start.7 = (bf16[4096,128]{1,0:T(8,128)(2,1)}, bf16[4096,128]{1,0:T(8,128)(2,1)S(1)}, u32[]{:S(2)}) copy-start(bf16[4096,128]{1,0:T(8,128)(2,1)S(1)} %collective-permute-done.7.refs_2_.refs_8_) | copy-start | bytes 3145732
  86.2 22.9 %collective-permute-start.13 = (bf16[4096,128]{1,0:T(8,128)(2,1)S(1)}, bf16[4096,128]{1,0:T(8,128)(2,1)}, u32[]{:S(2)}, u32[]{:S(2)}) collective-permute-start(bf16[4096,128]{1,0:T(8,128)(2,1)S(1)} %collective-permute-done.7.refs_2_.refs_8_), channel_id=1, source_target_pairs={{0,4},{1,13},{2,6},{3,15},{4,8},{5,1},{6,10},{7,3},{8,12},{9,5},{1... | collective-permute-start | bytes 3145736 | tf_op jit(solution)/shard_map/ppermute | solution.py:242
  88.2 34.1 %copy-start.8 = (bf16[4096,128]{1,0:T(8,128)(2,1)}, bf16[4096,128]{1,0:T(8,128)(2,1)S(1)}, u32[]{:S(2)}) copy-start(bf16[4096,128]{1,0:T(8,128)(2,1)S(1)} %collective-permute-done.4.refs_5_) | copy-start | bytes 3145732
  88.2 31.4 %collective-permute-start.8 = (bf16[4096,128]{1,0:T(8,128)(2,1)S(1)}, bf16[4096,128]{1,0:T(8,128)(2,1)S(1)}, u32[]{:S(2)}, u32[]{:S(2)}) collective-permute-start(bf16[4096,128]{1,0:T(8,128)(2,1)S(1)} %collective-permute-done.7.refs_2_.refs_8_), channel_id=1, source_target_pairs={{0,1},{1,0},{2,3},{3,2},{4,5},{5,4},{6,7},{7,6},{8,9},{9,8},{10,11... | collective-permute-start | bytes 3145736 | tf_op jit(solution)/shard_map/ppermute | solution.py:244
  104.7 16.2 %collective-permute-start.10 = (bf16[4096,128]{1,0:T(8,128)(2,1)S(1)}, bf16[4096,128]{1,0:T(8,128)(2,1)S(1)}, u32[]{:S(2)}, u32[]{:S(2)}) collective-permute-start(bf16[4096,128]{1,0:T(8,128)(2,1)S(1)} %collective-permute-done.9.refs_4_.refs_10_), channel_id=1, source_target_pairs={{0,1},{1,0},{2,3},{3,2},{4,5},{5,4},{6,7},{7,6},{8,9},{9,8},{10,11... | collective-permute-start | bytes 3145736 | tf_op jit(solution)/shard_map/ppermute | solution.py:244
  104.7 17.5 %collective-permute-start.20 = (bf16[4096,128]{1,0:T(8,128)(2,1)S(1)}, bf16[4096,128]{1,0:T(8,128)(2,1)}, u32[]{:S(2)}, u32[]{:S(2)}) collective-permute-start(bf16[4096,128]{1,0:T(8,128)(2,1)S(1)} %collective-permute-done.19.refs_10_), channel_id=1, source_target_pairs={{4,36},{6,38},{8,40},{10,42},{12,44},{13,109},{14,46},{15,111},{20... | collective-permute-start | bytes 3145736 | tf_op jit(solution)/shard_map/ppermute | solution.py:242
  106.1 27.1 %collective-permute-start.12 = (bf16[4096,128]{1,0:T(8,128)(2,1)}, bf16[4096,128]{1,0:T(8,128)(2,1)}, u32[]{:S(2)}, u32[]{:S(2)}) collective-permute-start(bf16[4096,128]{1,0:T(8,128)(2,1)} %collective-permute-done.11.refs_0_.refs_12_), channel_id=1, source_target_pairs={{0,1},{1,0},{2,3},{3,2},{4,5},{5,4},{6,7},{7,6},{8,9},{9,8},{10,11... | collective-permute-start | bytes 3145736 | tf_op jit(solution)/shard_map/ppermute | solution.py:244
  109.2 24.0 %collective-permute-start.14 = (bf16[4096,128]{1,0:T(8,128)(2,1)}, bf16[4096,128]{1,0:T(8,128)(2,1)}, u32[]{:S(2)}, u32[]{:S(2)}) collective-permute-start(bf16[4096,128]{1,0:T(8,128)(2,1)} %collective-permute-done.13.refs_6_.refs_14_), channel_id=1, source_target_pairs={{0,1},{1,0},{2,3},{3,2},{4,5},{5,4},{6,7},{7,6},{8,9},{9,8},{10,11... | collective-permute-start | bytes 3145736 | tf_op jit(solution)/shard_map/ppermute | solution.py:244
  119.6 25.6 %collective-permute-start.17 = (bf16[4096,128]{1,0:T(8,128)(2,1)}, bf16[4096,128]{1,0:T(8,128)(2,1)}, u32[]{:S(2)}, u32[]{:S(2)}) collective-permute-start(bf16[4096,128]{1,0:T(8,128)(2,1)} %collective-permute-done.16.refs_9_), channel_id=1, source_target_pairs={{4,36},{6,38},{8,40},{10,42},{12,44},{13,109},{14,46},{15,111},{22... | collective-permute-start | bytes 3145736 | tf_op jit(solution)/shard_map/ppermute | solution.py:242
  120.9 27.5 %collective-permute-start.18 = (bf16[4096,128]{1,0:T(8,128)(2,1)}, bf16[4096,128]{1,0:T(8,128)(2,1)}, u32[]{:S(2)}, u32[]{:S(2)}) collective-permute-start(bf16[4096,128]{1,0:T(8,128)(2,1)} %collective-permute-done.16.refs_9_), channel_id=1, source_target_pairs={{5,37},{7,39},{9,41},{11,43},{12,108},{13,45},{14,110},{15,47},{23... | collective-permute-start | bytes 3145736 | tf_op jit(solution)/shard_map/ppermute | solution.py:242
  122.3 26.1 %collective-permute-start.21 = (bf16[4096,128]{1,0:T(8,128)(2,1)}, bf16[4096,128]{1,0:T(8,128)(2,1)}, u32[]{:S(2)}, u32[]{:S(2)}) collective-permute-start(bf16[4096,128]{1,0:T(8,128)(2,1)} %collective-permute-done.20.refs_18_), channel_id=1, source_target_pairs={{2,18},{3,19},{4,20},{5,21},{6,22},{7,23},{8,24},{9,25},{10,26},{1... | collective-permute-start | bytes 3145736 | tf_op jit(solution)/shard_map/ppermute | solution.py:242
  (5 other events, 63.8 us)
